TPU v7x, 32 devices: a whole 2x2x4 slice. The times are simulated.
32 devices in a mesh: shard: 4 (over y, x), ctx: 2 (over core), tp: 4 (over z).
Axes of the slice: x: 2, y: 2, z: 4, core: 2. Of those that a mesh axis runs over, the one named last changes fastest.
Arguments:
- latents: bfloat16 [4, 2048, 1024], P('shard', 'ctx'), may hold values from -6 to 6
- condition: bfloat16 [4, 1024], P('shard'), may hold values from -6 to 6
- modulation_weight: bfloat16 [1024, 6, 1024], P(('shard', 'ctx'), None, 'tp'), may hold values from -0.1875 to 0.1875
- modulation_bias: bfloat16 [6, 1024], P(None, 'tp'), may hold values from -3 to 3
- heads_weight: bfloat16 [1024, 3, 1024], P(('shard', 'ctx'), None, 'tp'), may hold values from -0.1875 to 0.1875
- heads_bias: bfloat16 [2, 1024], P(None, 'tp'), may hold values from -1.25 to 1.25
- merge_weight: bfloat16 [1024, 1024], P(('shard', 'ctx'), 'tp'), may hold values from -0.75 to 0.75
- merge_bias: bfloat16 [1024], replicated, may hold values from -3 to 3
- expand_weight: bfloat16 [1024, 4096], P(('shard', 'ctx'), 'tp'), may hold values from -0.1875 to 0.1875
- expand_bias: bfloat16 [4096], P('tp'), may hold values from -3 to 3
- reduce_weight: bfloat16 [1024, 4096], P(('shard', 'ctx'), 'tp'), may hold values from -0.09375 to 0.09375
- reduce_bias: bfloat16 [1024], replicated, may hold values from -3 to 3
- cotangent: bfloat16 [4, 2048, 1024], P('shard', 'ctx'), may hold values from -6 to 6
Outputs:
- output: bfloat16 [4, 2048, 1024], P('shard', 'ctx')
- latents_grad: float32 [4, 2048, 1024], P('shard', 'ctx')
- modulation_weight_grad: float32 [1024, 6, 1024], P(('shard', 'ctx'), None, 'tp')
- modulation_bias_grad: float32 [6, 1024], P(None, 'tp')
- heads_weight_grad: float32 [1024, 3, 1024], P(('shard', 'ctx'), None, 'tp')
- heads_bias_grad: float32 [2, 1024], P(None, 'tp')
- merge_weight_grad: float32 [1024, 1024], P(('shard', 'ctx'), 'tp')
- merge_bias_grad: float32 [1024], replicated
- expand_weight_grad: float32 [1024, 4096], P(('shard', 'ctx'), 'tp')
- expand_bias_grad: float32 [4096], P('tp')
- reduce_weight_grad: float32 [1024, 4096], P(('shard', 'ctx'), 'tp')
- reduce_bias_grad: float32 [1024], replicated
All inputs are finite; a program needn't handle non-finite values.
Results may differ from a plain program's by a relative error of at most 0.018.
The roundings to bfloat16 on the way count: a program that leaves them out, or rounds other values in their place, can miss the bound.
Values may be sent and summed in bfloat16 or wider, within the bound.
No kernel may reach another device: no remote copies, remote signals or barrier semaphores. Data moves between devices by JAX's collectives and lax.ppermute only.
A program may use at most 192 MiB of HBM per device.

v0:
```python
import jax
import jax.numpy as jnp
from jax import lax
from jax.sharding import PartitionSpec as P

HD = 64


def modulate(values, offset, scaling):
    centre = values - jnp.mean(values, axis=-1, keepdims=True)
    variance = jnp.mean(centre * centre, axis=-1, keepdims=True)
    normed = centre * lax.rsqrt(variance + 1e-06)
    return normed * (1.0 + scaling[:, None, :]) + offset[:, None, :]


def smooth_gate(values):
    return jax.nn.gelu(values, approximate=True)


def split_heads(queries, key_value):
    count = queries.shape[-1] // HD
    query_heads = queries.reshape(queries.shape[0], count, HD)
    key_heads = key_value[:, 0].reshape(key_value.shape[0], count, HD)
    value_heads = key_value[:, 1].reshape(key_value.shape[0], count, HD)
    scores = jnp.einsum(
        "qhd,khd->hqk", query_heads, key_heads, preferred_element_type=jnp.float32
    ) * HD ** (-0.5)
    return (query_heads, key_heads, value_heads, scores)


def attend(inputs):
    queries, key_value = inputs
    query_heads, key_heads, value_heads, scores = split_heads(queries, key_value)
    maximum_entry = jnp.max(scores, axis=-1, keepdims=True)
    exponent = jnp.exp(scores - maximum_entry)
    summed = jnp.sum(exponent, axis=-1, keepdims=True)
    attention = (exponent / summed).astype(jnp.bfloat16)
    blended_heads = jnp.einsum(
        "hqk,khd->qhd", attention, value_heads, preferred_element_type=jnp.float32
    )
    blended_heads = blended_heads.reshape(queries.shape[0], queries.shape[1]).astype(jnp.bfloat16)
    log_total = maximum_entry[..., 0] + jnp.log(summed[..., 0])
    return (blended_heads, log_total)


def attend_back(inputs):
    queries, key_value, mixture_grad, log_total = inputs
    query_heads, key_heads, value_heads, scores = split_heads(queries, key_value)
    grad_heads = mixture_grad.reshape(query_heads.shape)
    weights = jnp.exp(scores - log_total[..., None])
    attention = weights.astype(jnp.bfloat16)
    probs_grad = jnp.einsum(
        "qhd,khd->hqk", grad_heads, value_heads, preferred_element_type=jnp.float32
    )
    row_dot = jnp.sum(weights * probs_grad, axis=-1, keepdims=True)
    score_grad = (weights * (probs_grad - row_dot)).astype(jnp.bfloat16)
    query_grad = jnp.einsum(
        "hqk,khd->qhd", score_grad, key_heads, preferred_element_type=jnp.float32
    ) * HD ** (-0.5)
    key_grad = jnp.einsum(
        "hqk,qhd->khd", score_grad, query_heads, preferred_element_type=jnp.float32
    ) * HD ** (-0.5)
    value_grad = jnp.einsum(
        "hqk,qhd->khd", attention, grad_heads, preferred_element_type=jnp.float32
    )
    width = queries.shape[1]
    stacked = jnp.stack(
        [
            key_grad.reshape(key_value.shape[0], width),
            value_grad.reshape(key_value.shape[0], width),
        ],
        axis=1,
    )
    return (query_grad.reshape(queries.shape[0], width), stacked)


def body(
    latents,
    condition,
    modulation_weight,
    modulation_bias,
    heads_weight,
    heads_bias,
    merge_weight,
    merge_bias,
    expand_weight,
    expand_bias,
    reduce_weight,
    reduce_bias,
    cotangent,
):
    silu_condition = jax.nn.silu(condition.astype(jnp.float32)).astype(jnp.bfloat16)
    gathered = (
        lax.all_gather(modulation_weight, ("shard", "ctx"), axis=0, tiled=True),
        lax.all_gather(heads_weight, ("shard", "ctx"), axis=0, tiled=True),
        lax.all_gather(merge_weight, ("shard", "ctx"), axis=0, tiled=True),
        lax.all_gather(expand_weight, ("shard", "ctx"), axis=0, tiled=True),
        lax.all_gather(reduce_weight, ("shard", "ctx"), axis=0, tiled=True),
    )
    complete_modulation, heads_full, merge_complete, expand_full, reduce_full = gathered
    local_modulation = jnp.einsum(
        "ld,dkf->lkf", silu_condition, complete_modulation, preferred_element_type=jnp.float32
    )
    local_modulation = local_modulation + modulation_bias.astype(jnp.float32)
    modulation = lax.all_gather(local_modulation, "tp", axis=2, tiled=True)
    offset_one = modulation[:, 0]
    scaling_one = modulation[:, 1]
    gate_one = modulation[:, 2]
    offset_two = modulation[:, 3]
    scaling_two = modulation[:, 4]
    gate_two = modulation[:, 5]
    residual = latents.astype(jnp.float32)
    normed_one = modulate(residual, offset_one, scaling_one).astype(jnp.bfloat16)
    projected = jnp.einsum(
        "lsd,dkf->lskf", normed_one, heads_full, preferred_element_type=jnp.float32
    )
    bias_rows = heads_bias.astype(jnp.float32)
    bias_full = jnp.stack([bias_rows[0], jnp.zeros_like(bias_rows[0]), bias_rows[1]])
    projected = (projected + bias_full).astype(jnp.bfloat16)
    queries = projected[:, :, 0]
    key_value = lax.all_gather(projected[:, :, 1:], "ctx", axis=1, tiled=True)
    blended_heads, log_total = lax.map(attend, (queries, key_value))
    merged_output = jnp.einsum(
        "vzm,tm->vzt", blended_heads, merge_complete, preferred_element_type=jnp.float32
    )
    branch_one = lax.psum(merged_output.astype(jnp.bfloat16), "tp").astype(
        jnp.float32
    ) + merge_bias.astype(jnp.float32)
    middle = residual + gate_one[:, None, :] * branch_one
    normed_two = modulate(middle, offset_two, scaling_two).astype(jnp.bfloat16)
    hidden = jnp.einsum("lsd,dh->lsh", normed_two, expand_full, preferred_element_type=jnp.float32)
    hidden = hidden + expand_bias.astype(jnp.float32)
    activated = smooth_gate(hidden).astype(jnp.bfloat16)
    reduced = jnp.einsum("lsh,dh->lsd", activated, reduce_full, preferred_element_type=jnp.float32)
    branch_two = lax.psum(reduced.astype(jnp.bfloat16), "tp").astype(
        jnp.float32
    ) + reduce_bias.astype(jnp.float32)
    output = (middle + gate_two[:, None, :] * branch_two).astype(jnp.bfloat16)
    heads_back, merge_backward, expand_back, reduce_back = (
        lax.all_gather(heads_weight, ("shard", "ctx"), axis=0, tiled=True),
        lax.all_gather(merge_weight, ("shard", "ctx"), axis=0, tiled=True),
        lax.all_gather(expand_weight, ("shard", "ctx"), axis=0, tiled=True),
        lax.all_gather(reduce_weight, ("shard", "ctx"), axis=0, tiled=True),
    )
    upstream = cotangent.astype(jnp.float32)
    gate_two_grad = jnp.sum(upstream * branch_two, axis=1)
    branch_two_grad = (gate_two[:, None, :] * upstream).astype(jnp.bfloat16)
    reduce_bias_grad = jnp.sum(branch_two_grad.astype(jnp.float32), axis=(0, 1))
    reduce_weight_grad = jnp.einsum(
        "lsd,lsh->dh", branch_two_grad, activated, preferred_element_type=jnp.float32
    )
    activated_grad = jnp.einsum(
        "lsd,dh->lsh", branch_two_grad, reduce_back, preferred_element_type=jnp.float32
    )
    gate_pullback = jax.vjp(smooth_gate, hidden)[1]
    hidden_grad = gate_pullback(activated_grad)[0].astype(jnp.bfloat16)
    expand_bias_grad = jnp.sum(hidden_grad.astype(jnp.float32), axis=(0, 1))
    expand_weight_grad = jnp.einsum(
        "lsd,lsh->dh", normed_two, hidden_grad, preferred_element_type=jnp.float32
    )
    normed_two_part = jnp.einsum(
        "lsh,dh->lsd", hidden_grad, expand_back, preferred_element_type=jnp.float32
    )
    normed_two_grad = lax.psum(normed_two_part.astype(jnp.bfloat16), "tp").astype(jnp.float32)
    second_pullback = jax.vjp(modulate, middle, offset_two, scaling_two)[1]
    middle_part, offset_two_grad, scaling_two_grad = second_pullback(normed_two_grad)
    middle_grad = upstream + middle_part
    gate_one_grad = jnp.sum(middle_grad * branch_one, axis=1)
    first_branch_gradient = (gate_one[:, None, :] * middle_grad).astype(jnp.bfloat16)
    merge_bias_grad = jnp.sum(first_branch_gradient.astype(jnp.float32), axis=(0, 1))
    merge_weight_grad = jnp.einsum(
        "tab,tav->bv", first_branch_gradient, blended_heads, preferred_element_type=jnp.float32
    )
    mixture_grad = jnp.einsum(
        "yhq,qt->yht", first_branch_gradient, merge_backward, preferred_element_type=jnp.float32
    ).astype(jnp.bfloat16)
    query_grad, key_value_grad = lax.map(attend_back, (queries, key_value, mixture_grad, log_total))
    local_key_value = lax.psum_scatter(
        key_value_grad.astype(jnp.bfloat16), "ctx", scatter_dimension=1, tiled=True
    ).astype(jnp.float32)
    projected_grad = jnp.concatenate([query_grad[:, :, None], local_key_value], axis=2).astype(
        jnp.bfloat16
    )
    query_bias_grad = jnp.sum(projected_grad[:, :, 0].astype(jnp.float32), axis=(0, 1))
    value_bias_grad = jnp.sum(projected_grad[:, :, 2].astype(jnp.float32), axis=(0, 1))
    heads_bias_grad = jnp.stack([query_bias_grad, value_bias_grad])
    heads_weight_grad = jnp.einsum(
        "lsd,lskf->dkf", normed_one, projected_grad, preferred_element_type=jnp.float32
    )
    normed_one_part = jnp.einsum(
        "lskf,dkf->lsd", projected_grad, heads_back, preferred_element_type=jnp.float32
    )
    normed_one_grad = lax.psum(normed_one_part.astype(jnp.bfloat16), "tp").astype(jnp.float32)
    first_pullback = jax.vjp(modulate, residual, offset_one, scaling_one)[1]
    residual_part, offset_one_grad, scaling_one_grad = first_pullback(normed_one_grad)
    latents_grad = middle_grad + residual_part
    modulation_grad = jnp.stack(
        [
            offset_one_grad,
            scaling_one_grad,
            gate_one_grad,
            offset_two_grad,
            scaling_two_grad,
            gate_two_grad,
        ],
        axis=1,
    )
    feature_width = local_modulation.shape[2]
    local_grad = lax.dynamic_slice_in_dim(
        modulation_grad, lax.axis_index("tp") * feature_width, feature_width, 2
    )
    modulation_bias_grad = jnp.sum(local_grad, axis=0)
    condition_wide = silu_condition.astype(jnp.float32)
    modulation_weight_grad = jnp.einsum(
        "ld,lkf->dkf", condition_wide, local_grad, precision=lax.Precision.HIGHEST
    )
    weight_parts = (
        lax.psum_scatter(modulation_weight_grad, ("shard", "ctx"), scatter_dimension=0, tiled=True),
        lax.psum_scatter(heads_weight_grad, ("shard", "ctx"), scatter_dimension=0, tiled=True),
        lax.psum_scatter(merge_weight_grad, ("shard", "ctx"), scatter_dimension=0, tiled=True),
        lax.psum_scatter(expand_weight_grad, ("shard", "ctx"), scatter_dimension=0, tiled=True),
        lax.psum_scatter(reduce_weight_grad, ("shard", "ctx"), scatter_dimension=0, tiled=True),
    )
    modulation_rows_grad = weight_parts[0]
    heads_part, merge_part, expand_part, reduce_part = (
        weight_parts[1],
        weight_parts[2],
        weight_parts[3],
        weight_parts[4],
    )
    bias_parts = lax.psum(
        (
            modulation_bias_grad,
            heads_bias_grad,
            merge_bias_grad,
            expand_bias_grad,
            reduce_bias_grad,
        ),
        ("shard", "ctx"),
    )
    return (
        output,
        latents_grad,
        modulation_rows_grad,
        bias_parts[0],
        heads_part,
        bias_parts[1],
        merge_part,
        bias_parts[2],
        expand_part,
        bias_parts[3],
        reduce_part,
        bias_parts[4],
    )


def solution(mesh):
    return jax.shard_map(
        body,
        mesh=mesh,
        in_specs=(
            P("shard", "ctx", None),
            P("shard", None),
            P(("shard", "ctx"), None, "tp"),
            P(None, "tp"),
            P(("shard", "ctx"), None, "tp"),
            P(None, "tp"),
            P(("shard", "ctx"), "tp"),
            P(),
            P(("shard", "ctx"), "tp"),
            P("tp"),
            P(("shard", "ctx"), "tp"),
            P(),
            P("shard", "ctx", None),
        ),
        out_specs=(
            P("shard", "ctx", None),
            P("shard", "ctx", None),
            P(("shard", "ctx"), None, "tp"),
            P(None, "tp"),
            P(("shard", "ctx"), None, "tp"),
            P(None, "tp"),
            P(("shard", "ctx"), "tp"),
            P(),
            P(("shard", "ctx"), "tp"),
            P("tp"),
            P(("shard", "ctx"), "tp"),
            P(),
        ),
        check_vma=False,
    )
```

profile of v0, /device:TPU:0, one launch (start us, length us, event | category | flops | bytes accessed | tf_op | source)
XLA Modules:
  0.0 929.9 jit_solution(7180096306416691299)
XLA Ops:
  8.0 1.7 copy.25
  9.9 1.9 convert_reduce_fusion.2
  13.4 31.6 %all-gather.7.cloned.1.call-done = bf16[1024,6,256]{2,0,1:T(8,128)(2,1)} async-done(((bf16[128,6,256]{2,0,1:T(8,128)(2,1)}), bf16[1024,6,256]{2,0,1:T(8,128)(2,1)}) %all-gather.7.cloned.1.call-update) | async-done | bytes 3145744 | tf_op jit(solution)/shard_map/all_gather | solution.py:94
  45.0 2.4 fusion.56
  47.4 13.2 %all-gather = f32[6,1024]{1,0:T(8,128)S(1)} all-gather(f32[6,256]{1,0:T(8,128)S(1)} %bitcast_add_fusion), channel_id=2, replica_groups=mesh['shard'=4,'ctx'=2,'tp'=4] {'tp'}, dimensions={1}, use_global_device_ids=true | all-gather | bytes 30720 | tf_op jit(solution)/shard_map/all_gather | solution.py:105
  60.6 12.7 %all-gather.9.cloned.1.call-done = bf16[1024,3,256]{0,2,1:T(8,128)(2,1)} async-done(((bf16[128,3,256]{0,2,1:T(8,128)(2,1)}), bf16[1024,3,256]{0,2,1:T(8,128)(2,1)}) %all-gather.9.cloned.1.call-update) | async-done | bytes 1572880 | tf_op jit(solution)/shard_map/all_gather | solution.py:95
  73.4 3.4 fusion.49
  79.1 11.3 %all_gather.29 = bf16[1024,256]{1,0:T(8,128)(2,1)} all-gather(bf16[128,256]{1,0:T(8,128)(2,1)S(1)} %copy-done.22), channel_id=1, replica_groups=mesh['shard'=4,'ctx'=2,'tp'=4] {'shard','ctx'}, dimensions={0}, use_global_device_ids=true | all-gather | bytes 589824 | tf_op jit(solution)/shard_map/all_gather | solution.py:96
  91.5 2.9 fusion.69
  94.4 13.1 %multiply_reduce_fusion.1 = (f32[4,1024]{1,0:T(4,128)S(1)}, f32[4,1024,2048]{2,1,0:T(8,128)}) fusion(bf16[1024,4,64]{0,2,1:T(8,128)(2,1)S(1)} %bitcast.106, bf16[2048,4,64]{0,2,1:T(8,128)(2,1)S(1)} %bitcast.108), kind=kOutput, calls=%fused_computation.6 | convolution fusion | flops 1090514944 | bytes 35143680 | tf_op jit(solution)/shard_map/while/body/eval_jaxpr/qhd,khd->hqk/dot_general | solution.py:25
  107.5 14.1 %fusion = f32[4,1024]{1,0:T(4,128)S(1)} fusion(f32[4,1024,2048]{2,1,0:T(8,128)} %get-tuple-element.81, f32[4,1024]{1,0:T(4,128)S(1)} %get-tuple-element.80), kind=kLoop, calls=%fused_computation.5 | loop fusion | flops 25161728 | bytes 33587200 | tf_op jit(solution)/shard_map/while/body/eval_jaxpr/reduce_sum | solution.py:36
  121.6 15.0 %fusion.54 = bf16[4,64,1024]{2,1,0:T(8,128)(2,1)} fusion(bf16[2048,4,64]{0,2,1:T(8,128)(2,1)S(1)} %bitcast.110, f32[4,1024,2048]{2,1,0:T(8,128)} %get-tuple-element.81, f32[4,1024]{1,0:T(4,128)S(1)} %fusion, f32[4,1024]{1,0:T(4,128)S(1)} %get-tuple-element.80), kind=kOutput, calls=%fused_computation.89 | convolution fusion | flops 1107558400 | bytes 35160064 | tf_op jit(solution)/shard_map/while/body/eval_jaxpr/hqk,khd->qhd/dot_general | solution.py:38
  136.6 3.3 convert_bitcast_fusion.2
  141.4 85.3 %all-reduce.6.cloned.1.call-done = bf16[1,1024,1024]{2,1,0:T(8,128)(2,1)} async-done(((bf16[1,1024,1024]{2,1,0:T(8,128)(2,1)}), bf16[1,1024,1024]{2,1,0:T(8,128)(2,1)}) %all-reduce.6.cloned.1.call-update) | async-done | bytes 2097168 | tf_op jit(solution)/shard_map/psum | solution.py:126
  226.6 2.6 fusion.65
  230.5 2.6 fusion.34
  233.1 22.3 %all-gather.13.cloned.1.call-done = bf16[1024,1024]{1,0:T(8,128)(2,1)} async-done(((bf16[128,1024]{1,0:T(8,128)(2,1)}), bf16[1024,1024]{1,0:T(8,128)(2,1)}) %all-gather.13.cloned.1.call-update) | async-done | bytes 2097168 | tf_op jit(solution)/shard_map/all_gather | solution.py:97
  255.4 6.6 fusion.72
  262.0 23.3 %all-gather.15.cloned.1.call-done = bf16[1024,1024]{1,0:T(8,128)(2,1)} async-done(((bf16[128,1024]{1,0:T(8,128)(2,1)}), bf16[1024,1024]{1,0:T(8,128)(2,1)}) %all-gather.15.cloned.1.call-update) | async-done | bytes 2097168 | tf_op jit(solution)/shard_map/all_gather | solution.py:98
  285.3 8.4 convert_reduce_fusion.4
  294.9 3.7 convert_bitcast_fusion
  298.9 86.4 %all-reduce.8.cloned.1.call-done = bf16[1,1024,1024]{2,1,0:T(8,128)(2,1)} async-done(((bf16[1,1024,1024]{2,1,0:T(8,128)(2,1)}), bf16[1,1024,1024]{2,1,0:T(8,128)(2,1)}) %all-reduce.8.cloned.1.call-update) | async-done | bytes 2097168 | tf_op jit(solution)/shard_map/psum | solution.py:164
  385.3 4.6 fusion.27
  390.0 2.5 fusion.68
  394.5 1.4 copy-done.8
  396.6 14.7 %fusion.31 = bf16[4,64,2048]{2,1,0:T(8,128)(2,1)} fusion(bf16[1024,4,64]{0,2,1:T(8,128)(2,1)S(1)} %bitcast.114, f32[4,1024,2048]{2,1,0:T(8,128)} %get-tuple-element.81, f32[4,1024]{1,0:T(4,128)S(1)} %log_add_fusion), kind=kOutput, calls=%fused_computation.68 | convolution fusion | flops 1099431936 | bytes 35143680 | tf_op jit(solution)/shard_map/while/body/eval_jaxpr/hqk,qhd->khd/dot_general | solution.py:63
  411.3 22.3 %multiply_reduce_fusion = (f32[4,1024]{1,0:T(4,128)S(1)}, f32[4,1024,2048]{2,1,0:T(8,128)}) fusion(f32[4,1024,2048]{2,1,0:T(8,128)} %get-tuple-element.81, f32[4,1024]{1,0:T(4,128)S(1)} %log_add_fusion, bf16[1024,4,64]{0,2,1:T(8,128)(2,1)S(1)} %bitcast.115, bf16[2048,4,64]{0,2,1:T(8,128)(2,1)S(1)} %bitcast.111), kind=kOutput, calls=%fused_computation.1 | convolution fusion | flops 1107292160 | bytes 68714496 | tf_op jit(solution)/shard_map/while/body/eval_jaxpr/qhd,khd->hqk/dot_general | solution.py:52
  433.6 2.3 copy.27
  435.8 28.2 %multiply_convert_fusion = bf16[4,1024,2048]{2,1,0:T(8,128)(2,1)} fusion(f32[4,1024,2048]{2,1,0:T(8,128)} %get-tuple-element.83, f32[4,1024,2048]{2,1,0:T(8,128)} %get-tuple-element.81, f32[4,1024]{1,0:T(4,128)S(1)} %get-tuple-element.82, f32[4,1024]{1,0:T(4,128)S(1)} %log_add_fusion), kind=kLoop, calls=%fused_computation | loop fusion | flops 41943040 | bytes 83918848 | tf_op jit(solution)/shard_map/while/body/eval_jaxpr/convert_element_type | solution.py:56
  464.0 9.0 fusion.30
  474.3 3.0 pad_maximum_fusion
  477.4 7.1 convert_bitcast_fusion.1
  484.5 12.0 %convert_reduce_fusion.6 = (f32[4,64]{1,0:T(4,128)S(1)}, bf16[4,64,1024]{2,1,0:T(8,128)(2,1)}) fusion(bf16[2048,4,64]{0,2,1:T(8,128)(2,1)S(1)} %bitcast.109, bf16[4,1024,2048]{2,1,0:T(8,128)(2,1)} %multiply_convert_fusion), kind=kOutput, calls=%fused_computation.90 | convolution fusion | flops 1074790144 | bytes 18351104 | tf_op jit(solution)/shard_map/while/body/eval_jaxpr/hqk,khd->qhd/dot_general | solution.py:57
  497.8 4.9 fusion.46
  503.7 3.3 fusion.36
  507.3 7.0 fusion.73
  514.3 7.5 fusion.40
  522.5 5.0 fusion.55
  527.8 129.6 %all-reduce.10.cloned.1.call-done = (bf16[1,1024,1024]{2,1,0:T(8,128)(2,1)}, bf16[1,1024,1024]{2,1,0:T(8,128)(2,1)}) async-done(((bf16[1,1024,1024]{2,1,0:T(8,128)(2,1)}, bf16[1,1024,1024]{2,1,0:T(8,128)(2,1)}), (bf16[1,1024,1024]{2,1,0:T(8,128)(2,1)}, bf16[1,1024,1024]{2,1,0:T(8,128)(2,1)})) %all-reduce.10.cloned.1.call-update) | async-done | bytes 4194320 | tf_op jit(solution)/shard_map/psum | solution.py:135
  657.4 2.7 fusion.24
  660.1 2.6 fusion.28
  662.8 7.9 convert_reduce_fusion.3
  670.7 3.1 broadcast_multiply_fusion
  675.2 24.8 %all-reduce = (f32[6,256]{1,0:T(8,128)}, f32[2,256]{1,0:T(2,128)}, f32[1024]{0:T(1024)}, f32[1024]{0:T(1024)}, f32[1024]{0:T(1024)}) all-reduce(f32[6,256]{1,0:T(8,128)S(1)} %dynamic-slice_bitcast_fusion, f32[2,256]{1,0:T(2,128)S(1)} %pad_maximum_fusion.5, ...), channel_id=1, replica_groups=mesh['shard'=4,'ctx'=2,'tp'=4] {'shard','ctx'}, use_global_device_ids=true, to_apply=%region_23.24 | all-reduce | flops 5120 | bytes 40960 | tf_op jit(solution)/shard_map/psum | solution.py:231
  700.0 51.5 %reduce-scatter.15.cloned.1.call-done = f32[128,1024]{1,0:T(8,128)} async-done(((f32[1024,1024]{1,0:T(8,128)}), f32[128,1024]{1,0:T(8,128)}) %reduce-scatter.15.cloned.1.call-update) | async-done | bytes 524304 | tf_op jit(solution)/shard_map/reduce_scatter | solution.py:221
  751.5 55.5 %reduce-scatter.17.cloned.1.call-done = f32[128,1024]{1,0:T(8,128)} async-done(((f32[1024,1024]{1,0:T(8,128)}), f32[128,1024]{1,0:T(8,128)}) %reduce-scatter.17.cloned.1.call-update) | async-done | bytes 524304 | tf_op jit(solution)/shard_map/reduce_scatter | solution.py:222
  807.0 50.2 %reduce-scatter.11.cloned.1.call-done = f32[128,3,256]{2,0,1:T(8,128)} async-done(((f32[1024,3,256]{2,0,1:T(8,128)}), f32[128,3,256]{2,0,1:T(8,128)}) %reduce-scatter.11.cloned.1.call-update) | async-done | bytes 393232 | tf_op jit(solution)/shard_map/reduce_scatter | solution.py:219
  857.2 66.0 %reduce-scatter.9.cloned.1.call-done = f32[128,6,256]{2,0,1:T(8,128)} async-done(((f32[1024,6,256]{2,0,1:T(8,128)}), f32[128,6,256]{2,0,1:T(8,128)}) %reduce-scatter.9.cloned.1.call-update) | async-done | bytes 786448 | tf_op jit(solution)/shard_map/reduce_scatter | solution.py:218
  (136 shorter events, 19.0 us)
Async XLA Ops:
  7.2 5.5 copy-start
  7.2 37.8 %copy-start.27 = (bf16[1,1024]{1,0:T(2,128)(2,1)S(1)}, bf16[1,1024]{1,0:T(2,128)(2,1)}, u32[]{:S(2)}) copy-start(bf16[1,1024]{1,0:T(2,128)(2,1)} %param.14) | copy-start | bytes 6148
  7.2 40.2 %copy-start.31 = (bf16[6,256]{1,0:T(8,128)(2,1)S(1)}, bf16[6,256]{1,0:T(8,128)(2,1)}, u32[]{:S(2)}) copy-start(bf16[6,256]{1,0:T(8,128)(2,1)} %param.16) | copy-start | bytes 9220
  7.2 37.8 %all-gather.7.cloned.1.call-start = ((), (), s32[]{:S(2)}) async-start(), calls=%async_computation.6 | async-start | bytes 3538944 | tf_op jit(solution)/shard_map/all_gather | solution.py:94
  7.9 65.4 %all-gather.9.cloned.1.call-start = ((), (), s32[]{:S(2)}) async-start(), calls=%async_computation.7 | async-start | bytes 1769472 | tf_op jit(solution)/shard_map/all_gather | solution.py:95
  9.8 81.8 %all-gather.11.cloned.1.call-start = ((), (), s32[]{:S(2)}) async-start(), calls=%async_computation.8 | async-start | bytes 3145728 | tf_op jit(solution)/shard_map/all_gather | solution.py:121
  12.7 64.1 %copy-start.18 = (f32[1024]{0:T(1024)}, f32[1024]{0:T(1024)S(1)}, u32[]{:S(2)}) copy-start(f32[1024]{0:T(1024)S(1)} %broadcast_multiply_fusion.2) | copy-start | bytes 12292
  13.3 34.1 %copy-start.25 = (f32[1024]{0:T(1024)}, f32[1024]{0:T(1024)S(1)}, u32[]{:S(2)}) copy-start(f32[1024]{0:T(1024)S(1)} %fusion.23) | copy-start | bytes 12292
  13.4 63.4 %copy-start.23 = (f32[1024]{0:T(1024)}, f32[1024]{0:T(1024)S(1)}, u32[]{:S(2)}) copy-start(f32[1024]{0:T(1024)S(1)} %fusion.59) | copy-start | bytes 12292
  60.6 16.2 %copy-start.20 = (f32[1,1,1024]{2,1,0:T(1,128)}, f32[1,1,1024]{2,1,0:T(1,128)S(1)}, u32[]{:S(2)}) copy-start(f32[1,1,1024]{2,1,0:T(1,128)S(1)} %get-tuple-element.76) | copy-start | bytes 12292
  60.6 16.2 %copy-start.29 = (f32[1,1,1024]{2,1,0:T(1,128)}, f32[1,1,1024]{2,1,0:T(1,128)S(1)}, u32[]{:S(2)}) copy-start(f32[1,1,1024]{2,1,0:T(1,128)S(1)} %get-tuple-element.75) | copy-start | bytes 12292
  73.4 5.7 copy-start.22
  76.8 1.1 copy-start.16
  79.1 147.6 %all-reduce.6.cloned.1.call-start = ((), (), s32[]{:S(2)}) async-start(), calls=%async_computation.9 | async-start | bytes 4194304 | tf_op jit(solution)/shard_map/psum | solution.py:126
  91.5 16.0 %copy-start.6 = (bf16[1,1024,1,256]{1,3,2,0:T(8,128)(2,1)}, bf16[1,1024,1,256]{1,3,2,0:T(8,128)(2,1)S(1)}, u32[]{:S(2)}) copy-start(bf16[1,1024,1,256]{1,3,2,0:T(8,128)(2,1)S(1)} %slice.67) | copy-start | bytes 1572868
  94.4 13.1 %copy-start.9 = (bf16[2048,1,256]{0,2,1:T(8,128)(2,1)}, bf16[2048,1,256]{0,2,1:T(8,128)(2,1)S(1)}, u32[]{:S(2)}) copy-start(bf16[2048,1,256]{0,2,1:T(8,128)(2,1)S(1)} %get-tuple-element.70) | copy-start | bytes 3145732
  107.5 14.1 %copy-start.13 = (bf16[2048,1,256]{0,2,1:T(8,128)(2,1)S(1)}, bf16[2048,1,256]{0,2,1:T(8,128)(2,1)}, u32[]{:S(2)}) copy-start(bf16[2048,1,256]{0,2,1:T(8,128)(2,1)} %get-tuple-element.71) | copy-start | bytes 3145732
  136.6 4.7 copy-start.32
  136.6 4.7 copy-start.33
  139.9 115.5 %all-gather.13.cloned.1.call-start = ((), (), s32[]{:S(2)}) async-start(), calls=%async_computation.10 | async-start | bytes 2359296 | tf_op jit(solution)/shard_map/all_gather | solution.py:97
  140.5 144.7 %all-gather.15.cloned.1.call-start = ((), (), s32[]{:S(2)}) async-start(), calls=%async_computation.11 | async-start | bytes 2359296 | tf_op jit(solution)/shard_map/all_gather | solution.py:98
  141.1 244.2 %all-reduce.8.cloned.1.call-start = ((), (), s32[]{:S(2)}) async-start(), calls=%async_computation.12 | async-start | bytes 4194304 | tf_op jit(solution)/shard_map/psum | solution.py:164
  226.6 2.6 copy-start.1
  285.3 9.7 %copy-start.35 = (bf16[1024,1024]{1,0:T(8,128)(2,1)S(1)}, bf16[1024,1024]{1,0:T(8,128)(2,1)}, u32[]{:S(2)}) copy-start(bf16[1024,1024]{1,0:T(8,128)(2,1)} %all-gather.13.cloned.1.call-done) | copy-start | bytes 6291460
  293.6 1.3 copy-start.36
  298.6 199.2 %reduce-scatter.7.cloned.1.call-start = ((), (), s32[]{:S(2)}) async-start(), calls=%async_computation.13 | async-start | bytes 3145728 | tf_op jit(solution)/shard_map/reduce_scatter | solution.py:178
  385.3 4.6 copy-start.2
  385.3 4.6 copy-start.12
  390.0 2.6 copy-start.11
  392.5 2.0 copy-start.4
  392.5 3.3 copy-start.15
  394.5 1.4 copy-start.8
  477.4 7.2 copy-start.10
  477.4 180.0 %all-reduce.10.cloned.1.call-start = ((), (), s32[]{:S(2)}) async-start(), calls=%async_computation.19 | async-start | bytes 8388608 | tf_op jit(solution)/shard_map/psum | solution.py:135
  502.7 1.0 copy-start.14
  502.7 197.3 %reduce-scatter.13.cloned.1.call-start = ((), (), s32[]{:S(2)}) async-start(), calls=%async_computation.16 | async-start | bytes 1179648 | tf_op jit(solution)/shard_map/reduce_scatter | solution.py:220
  507.1 244.4 %reduce-scatter.15.cloned.1.call-start = ((), (), s32[]{:S(2)}) async-start(), calls=%async_computation.17 | async-start | bytes 4718592 | tf_op jit(solution)/shard_map/reduce_scatter | solution.py:221
  514.3 292.7 %reduce-scatter.17.cloned.1.call-start = ((), (), s32[]{:S(2)}) async-start(), calls=%async_computation.18 | async-start | bytes 4718592 | tf_op jit(solution)/shard_map/reduce_scatter | solution.py:222
  521.8 0.7 copy-start.30
  521.9 5.8 copy-start.28
  521.9 5.9 copy-start.34
  521.9 335.3 %reduce-scatter.11.cloned.1.call-start = ((), (), s32[]{:S(2)}) async-start(), calls=%async_computation.15 | async-start | bytes 3538944 | tf_op jit(solution)/shard_map/reduce_scatter | solution.py:219
  527.6 132.5 %copy-start.26 = (f32[1024]{0:T(1024)S(1)}, f32[1024]{0:T(1024)}, u32[]{:S(2)}) copy-start(f32[1024]{0:T(1024)} %copy-done.25) | copy-start | bytes 12292
  527.6 395.6 %reduce-scatter.9.cloned.1.call-start = ((), (), s32[]{:S(2)}) async-start(), calls=%async_computation.14 | async-start | bytes 7077888 | tf_op jit(solution)/shard_map/reduce_scatter | solution.py:218
  657.4 2.8 copy-start.7
  657.4 5.4 copy-start.3
  657.4 5.4 copy-start.5
  673.9 1.2 copy-start.17
  (3 other events, 2.1 us)
Sparse Core Ops, SparseCore 0:
  9.9 35.0 all-gather.6
  47.4 25.8 all-gather.8
  79.2 10.5 all-gather.10
  140.1 86.5 all-reduce.5
  228.5 26.8 all-gather.12
  257.3 27.8 all-gather.14
  298.8 86.5 all-reduce.7
  477.5 8.5 reduce-scatter.6
  502.8 154.5 all-reduce.9
  661.0 35.2 reduce-scatter.12
  700.2 51.2 reduce-scatter.14
  755.6 51.2 reduce-scatter.16
  810.9 46.2 reduce-scatter.10
  861.4 61.7 reduce-scatter.8
where the time goes:
time: 934 us; the launch traced here: 930 us
  waiting for transfers between devices  616 us (66%)
  matrix products  149 us (16%)
  other arithmetic  79 us (8%)
  blocking collectives  49.2 us (5%)
  local copies, waits for them, and re-layouts  20.2 us (2%)
  between operations  14.6 us (2%)
    psum x1, waiting for transfers between devices, body(): lax.psum(reduced.astype(jnp.bfloat16), 'tp').astype(jnp.float32)  130 us
    psum x1, waiting for transfers between devices, body(): lax.psum(normed_two_part.astype(jnp.bfloat16), 'tp').astype(jnp.float32)  86.4 us
    psum x1, waiting for transfers between devices, body(): lax.psum(merged_output.astype(jnp.bfloat16), 'tp').astype(jnp.float32)  85.3 us
    reduce_scatter x1, waiting for transfers between devices, body(): lax.psum_scatter(modulation_weight_grad, ('shard', 'ctx'), scatter_dimens...  66 us
    reduce_scatter x1, waiting for transfers between devices, body(): lax.psum_scatter(reduce_weight_grad, ('shard', 'ctx'), scatter_dimension=...  55.5 us
    reduce_scatter x1, waiting for transfers between devices, body(): lax.psum_scatter(expand_weight_grad, ('shard', 'ctx'), scatter_dimension=...  51.5 us
    reduce_scatter x1, waiting for transfers between devices, body(): lax.psum_scatter(heads_weight_grad, ('shard', 'ctx'), scatter_dimension=0...  50.2 us
    all_gather x1, waiting for transfers between devices, body(): lax.all_gather(modulation_weight, ('shard', 'ctx'), axis=0, tiled=True)  31.6 us
  transfers between devices with their start and end apart: 14, of which 11 were waited for; matrix products, arithmetic and copies ran while one was open for 9% of the time, Pallas kernels for 0%

commit v1 on v0

--- a/solution.py
+++ b/solution.py
@@ -132,7 +132,7 @@
     hidden = hidden + expand_bias.astype(jnp.float32)
     activated = smooth_gate(hidden).astype(jnp.bfloat16)
     reduced = jnp.einsum("lsh,dh->lsd", activated, reduce_full, preferred_element_type=jnp.float32)
-    branch_two = lax.psum(reduced.astype(jnp.bfloat16), "tp").astype(
+    branch_two = jnp.sum(lax.all_gather(reduced.astype(jnp.bfloat16), "tp"), axis=0).astype(
         jnp.float32
     ) + reduce_bias.astype(jnp.float32)
     output = (middle + gate_two[:, None, :] * branch_two).astype(jnp.bfloat16)

time: 934 us -> 1010 us (1.081)
  waiting for transfers between devices: 616 us -> 684 us
  other arithmetic: 79 us -> 91.1 us
    all_gather x0 -> x1, waiting for transfers between devices: none -> 142 us  [body(): lax.all_gather(reduced.astype(jnp.bfloat16), 'tp')]
    psum x1, waiting for transfers between devices: 130 us -> 60.7 us  [body(): lax.psum(normed_one_part.astype(jnp.bfloat16), 'tp').astype(jnp.float32)]
    reduce_scatter x1, waiting for transfers between devices: 0.01 us -> 39.8 us  [body(): lax.psum_scatter(merge_weight_grad, ('shard', 'ctx'), scatter_dimension=0...]
    reduce_scatter x1, waiting for transfers between devices: 51.5 us -> 13.7 us  [body(): lax.psum_scatter(expand_weight_grad, ('shard', 'ctx'), scatter_dimension=...]
  transfers between devices with their start and end apart: 14 -> 15, of which waited for: 11 -> 13; matrix products, arithmetic and copies ran while one was open for 9% -> 9% of each run, Pallas kernels for 0% -> 0%
where the time goes in v1:
time: 1010 us
  waiting for transfers between devices  684 us (68%)
  matrix products  150 us (15%)
  other arithmetic  91.1 us (9%)
  blocking collectives  49.4 us (5%)
  local copies, waits for them, and re-layouts  19.1 us (2%)
  between operations  14.6 us (1%)
    all_gather x1, waiting for transfers between devices, body(): lax.all_gather(reduced.astype(jnp.bfloat16), 'tp')  142 us
    psum x1, waiting for transfers between devices, body(): lax.psum(merged_output.astype(jnp.bfloat16), 'tp').astype(jnp.float32)  85.3 us
    psum x1, waiting for transfers between devices, body(): lax.psum(normed_two_part.astype(jnp.bfloat16), 'tp').astype(jnp.float32)  79.3 us
    reduce_scatter x1, waiting for transfers between devices, body(): lax.psum_scatter(modulation_weight_grad, ('shard', 'ctx'), scatter_dimens...  65.9 us
    psum x1, waiting for transfers between devices, body(): lax.psum(normed_one_part.astype(jnp.bfloat16), 'tp').astype(jnp.float32)  60.7 us
    reduce_scatter x1, waiting for transfers between devices, body(): lax.psum_scatter(reduce_weight_grad, ('shard', 'ctx'), scatter_dimension=...  55.5 us
    reduce_scatter x1, waiting for transfers between devices, body(): lax.psum_scatter(heads_weight_grad, ('shard', 'ctx'), scatter_dimension=0...  50 us
    reduce_scatter x1, waiting for transfers between devices, body(): lax.psum_scatter(merge_weight_grad, ('shard', 'ctx'), scatter_dimension=0...  39.8 us
  transfers between devices with their start and end apart: 15, of which 13 were waited for; matrix products, arithmetic and copies ran while one was open for 9% of the time, Pallas kernels for 0%

profile of v1, /device:TPU:0, one launch (start us, length us, event | category | flops | bytes accessed | tf_op | source)
XLA Modules:
  0.0 1008.7 jit_solution(7253822820920419945)
XLA Ops:
  14.0 31.0 %all-gather.9.cloned.1.call-done = bf16[1024,6,256]{2,0,1:T(8,128)(2,1)} async-done(((bf16[128,6,256]{2,0,1:T(8,128)(2,1)}), bf16[1024,6,256]{2,0,1:T(8,128)(2,1)}) %all-gather.9.cloned.1.call-update) | async-done | bytes 3145744 | tf_op jit(solution)/shard_map/all_gather | solution.py:94
  45.0 2.4 fusion.59
  47.4 13.1 %all-gather = f32[6,1024]{1,0:T(8,128)S(1)} all-gather(f32[6,256]{1,0:T(8,128)S(1)} %bitcast_add_fusion), channel_id=2, replica_groups=mesh['shard'=4,'ctx'=2,'tp'=4] {'tp'}, dimensions={1}, use_global_device_ids=true | all-gather | bytes 30720 | tf_op jit(solution)/shard_map/all_gather | solution.py:105
  60.6 12.8 %all-gather.11.cloned.1.call-done = bf16[1024,3,256]{0,2,1:T(8,128)(2,1)} async-done(((bf16[128,3,256]{0,2,1:T(8,128)(2,1)}), bf16[1024,3,256]{0,2,1:T(8,128)(2,1)}) %all-gather.11.cloned.1.call-update) | async-done | bytes 1572880 | tf_op jit(solution)/shard_map/all_gather | solution.py:95
  73.4 3.4 fusion.52
  79.1 11.3 %all_gather.35 = bf16[1024,256]{1,0:T(8,128)(2,1)} all-gather(bf16[128,256]{1,0:T(8,128)(2,1)S(1)} %copy-done.16), channel_id=1, replica_groups=mesh['shard'=4,'ctx'=2,'tp'=4] {'shard','ctx'}, dimensions={0}, use_global_device_ids=true | all-gather | bytes 589824 | tf_op jit(solution)/shard_map/all_gather | solution.py:96
  91.5 2.9 fusion.72
  94.4 13.1 %multiply_reduce_fusion.1 = (f32[4,1024]{1,0:T(4,128)S(1)}, f32[4,1024,2048]{2,1,0:T(8,128)}) fusion(bf16[1024,4,64]{0,2,1:T(8,128)(2,1)S(1)} %bitcast.109, bf16[2048,4,64]{0,2,1:T(8,128)(2,1)S(1)} %bitcast.111), kind=kOutput, calls=%fused_computation.6 | convolution fusion | flops 1090514944 | bytes 35143680 | tf_op jit(solution)/shard_map/while/body/eval_jaxpr/qhd,khd->hqk/dot_general | solution.py:25
  107.5 14.1 %fusion = f32[4,1024]{1,0:T(4,128)S(1)} fusion(f32[4,1024,2048]{2,1,0:T(8,128)} %get-tuple-element.80, f32[4,1024]{1,0:T(4,128)S(1)} %get-tuple-element.79), kind=kLoop, calls=%fused_computation.5 | loop fusion | flops 25161728 | bytes 33587200 | tf_op jit(solution)/shard_map/while/body/eval_jaxpr/reduce_sum | solution.py:36
  121.6 15.0 %fusion.57 = bf16[4,64,1024]{2,1,0:T(8,128)(2,1)} fusion(bf16[2048,4,64]{0,2,1:T(8,128)(2,1)S(1)} %bitcast.114, f32[4,1024,2048]{2,1,0:T(8,128)} %get-tuple-element.80, f32[4,1024]{1,0:T(4,128)S(1)} %fusion, f32[4,1024]{1,0:T(4,128)S(1)} %get-tuple-element.79), kind=kOutput, calls=%fused_computation.91 | convolution fusion | flops 1107558400 | bytes 35160064 | tf_op jit(solution)/shard_map/while/body/eval_jaxpr/hqk,khd->qhd/dot_general | solution.py:38
  136.5 3.3 convert_bitcast_fusion.1
  141.3 85.3 %all-reduce.5.cloned.1.call-done = bf16[1,1024,1024]{2,1,0:T(8,128)(2,1)} async-done(((bf16[1,1024,1024]{2,1,0:T(8,128)(2,1)}), bf16[1,1024,1024]{2,1,0:T(8,128)(2,1)}) %all-reduce.5.cloned.1.call-update) | async-done | bytes 2097168 | tf_op jit(solution)/shard_map/psum | solution.py:126
  226.6 2.6 fusion.68
  230.4 2.7 fusion.37
  233.1 22.2 %all-gather.15.cloned.1.call-done = bf16[1024,1024]{1,0:T(8,128)(2,1)} async-done(((bf16[128,1024]{1,0:T(8,128)(2,1)}), bf16[1024,1024]{1,0:T(8,128)(2,1)}) %all-gather.15.cloned.1.call-update) | async-done | bytes 2097168 | tf_op jit(solution)/shard_map/all_gather | solution.py:97
  255.4 6.6 fusion.75
  261.9 23.3 %all-gather.17.cloned.1.call-done = bf16[1024,1024]{1,0:T(8,128)(2,1)} async-done(((bf16[128,1024]{1,0:T(8,128)(2,1)}), bf16[1024,1024]{1,0:T(8,128)(2,1)}) %all-gather.17.cloned.1.call-update) | async-done | bytes 2097168 | tf_op jit(solution)/shard_map/all_gather | solution.py:98
  285.2 8.4 convert_reduce_fusion.4
  294.9 3.7 convert_bitcast_fusion
  298.9 7.0 convolution_convert_fusion
  305.9 79.3 %all-reduce.7.cloned.1.call-done = bf16[1,1024,1024]{2,1,0:T(8,128)(2,1)} async-done(((bf16[1,1024,1024]{2,1,0:T(8,128)(2,1)}), bf16[1,1024,1024]{2,1,0:T(8,128)(2,1)}) %all-reduce.7.cloned.1.call-update) | async-done | bytes 2097168 | tf_op jit(solution)/shard_map/psum | solution.py:164
  385.3 4.2 fusion.27
  389.5 3.8 fusion.71
  393.3 142.1 %all-gather.19.cloned.1.call-done = bf16[4096,1024]{1,0:T(8,128)(2,1)} async-done(((bf16[1024,1024]{1,0:T(8,128)(2,1)}), bf16[4096,1024]{1,0:T(8,128)(2,1)}) %all-gather.19.cloned.1.call-update) | async-done | bytes 8388624 | tf_op jit(solution)/shard_map/all_gather | solution.py:135
  535.4 7.4 reduce.22
  542.9 6.9 convert_reduce_fusion.3
  551.9 14.7 %fusion.34 = bf16[4,64,2048]{2,1,0:T(8,128)(2,1)} fusion(bf16[1024,4,64]{0,2,1:T(8,128)(2,1)S(1)} %bitcast.118, f32[4,1024,2048]{2,1,0:T(8,128)} %get-tuple-element.80, f32[4,1024]{1,0:T(4,128)S(1)} %log_add_fusion), kind=kOutput, calls=%fused_computation.70 | convolution fusion | flops 1099431936 | bytes 35143680 | tf_op jit(solution)/shard_map/while/body/eval_jaxpr/hqk,qhd->khd/dot_general | solution.py:63
  566.6 22.8 %multiply_reduce_fusion = (f32[4,1024]{1,0:T(4,128)S(1)}, f32[4,1024,2048]{2,1,0:T(8,128)}) fusion(f32[4,1024,2048]{2,1,0:T(8,128)} %get-tuple-element.80, f32[4,1024]{1,0:T(4,128)S(1)} %log_add_fusion, bf16[1024,4,64]{0,2,1:T(8,128)(2,1)S(1)} %bitcast.119, bf16[2048,4,64]{0,2,1:T(8,128)(2,1)S(1)} %bitcast.115), kind=kOutput, calls=%fused_computation.1 | convolution fusion | flops 1107292160 | bytes 68714496 | tf_op jit(solution)/shard_map/while/body/eval_jaxpr/qhd,khd->hqk/dot_general | solution.py:52
  591.6 27.8 %multiply_convert_fusion = bf16[4,1024,2048]{2,1,0:T(8,128)(2,1)} fusion(f32[4,1024,2048]{2,1,0:T(8,128)} %get-tuple-element.82, f32[4,1024,2048]{2,1,0:T(8,128)} %get-tuple-element.80, f32[4,1024]{1,0:T(4,128)S(1)} %get-tuple-element.81, f32[4,1024]{1,0:T(4,128)S(1)} %log_add_fusion), kind=kLoop, calls=%fused_computation | loop fusion | flops 41943040 | bytes 83918848 | tf_op jit(solution)/shard_map/while/body/eval_jaxpr/convert_element_type | solution.py:56
  619.4 9.0 fusion.33
  629.7 3.2 pad_maximum_fusion
  633.0 12.5 %convert_reduce_fusion.6 = (f32[4,64]{1,0:T(4,128)S(1)}, bf16[4,64,1024]{2,1,0:T(8,128)(2,1)}) fusion(bf16[2048,4,64]{0,2,1:T(8,128)(2,1)S(1)} %bitcast.112, bf16[4,1024,2048]{2,1,0:T(8,128)(2,1)} %multiply_convert_fusion), kind=kOutput, calls=%fused_computation.92 | convolution fusion | flops 1074790144 | bytes 18351104 | tf_op jit(solution)/shard_map/while/body/eval_jaxpr/hqk,khd->qhd/dot_general | solution.py:57
  646.7 4.9 fusion.49
  651.8 6.6 fusion.76
  658.6 7.5 fusion.43
  667.0 3.4 fusion.39
  670.5 5.0 fusion.58
  675.7 60.7 %all-reduce.9.cloned.1.call-done = bf16[1,1024,1024]{2,1,0:T(8,128)(2,1)} async-done(((bf16[1,1024,1024]{2,1,0:T(8,128)(2,1)}), bf16[1,1024,1024]{2,1,0:T(8,128)(2,1)}) %all-reduce.9.cloned.1.call-update) | async-done | bytes 2097168 | tf_op jit(solution)/shard_map/psum | solution.py:193
  736.4 2.7 fusion.24
  739.2 2.6 fusion.28
  741.8 3.1 broadcast_multiply_fusion
  746.4 25.0 %all-reduce = (f32[6,256]{1,0:T(8,128)}, f32[2,256]{1,0:T(2,128)}, f32[1024]{0:T(1024)}, f32[1024]{0:T(1024)}, f32[1024]{0:T(1024)}) all-reduce(f32[6,256]{1,0:T(8,128)S(1)} %dynamic-slice_bitcast_fusion, f32[2,256]{1,0:T(2,128)S(1)} %pad_maximum_fusion.5, ...), channel_id=1, replica_groups=mesh['shard'=4,'ctx'=2,'tp'=4] {'shard','ctx'}, use_global_device_ids=true, to_apply=%region_23.24 | all-reduce | flops 5120 | bytes 40960 | tf_op jit(solution)/shard_map/psum | solution.py:231
  771.3 5.8 add_add_fusion.2
  777.1 13.7 %reduce-scatter.15.cloned.1.call-done = f32[128,1024]{1,0:T(8,128)} async-done(((f32[1024,1024]{1,0:T(8,128)}), f32[128,1024]{1,0:T(8,128)}) %reduce-scatter.15.cloned.1.call-update) | async-done | bytes 524304 | tf_op jit(solution)/shard_map/reduce_scatter | solution.py:221
  790.8 55.5 %reduce-scatter.17.cloned.1.call-done = f32[128,1024]{1,0:T(8,128)} async-done(((f32[1024,1024]{1,0:T(8,128)}), f32[128,1024]{1,0:T(8,128)}) %reduce-scatter.17.cloned.1.call-update) | async-done | bytes 524304 | tf_op jit(solution)/shard_map/reduce_scatter | solution.py:222
  846.3 39.8 %reduce-scatter.13.cloned.1.call-done = f32[128,256]{1,0:T(8,128)} async-done(((f32[1024,256]{1,0:T(8,128)}), f32[128,256]{1,0:T(8,128)}) %reduce-scatter.13.cloned.1.call-update) | async-done | bytes 131088 | tf_op jit(solution)/shard_map/reduce_scatter | solution.py:220
  886.0 50.0 %reduce-scatter.11.cloned.1.call-done = f32[128,3,256]{2,0,1:T(8,128)} async-done(((f32[1024,3,256]{2,0,1:T(8,128)}), f32[128,3,256]{2,0,1:T(8,128)}) %reduce-scatter.11.cloned.1.call-update) | async-done | bytes 393232 | tf_op jit(solution)/shard_map/reduce_scatter | solution.py:219
  936.1 65.9 %reduce-scatter.9.cloned.1.call-done = f32[128,6,256]{2,0,1:T(8,128)} async-done(((f32[1024,6,256]{2,0,1:T(8,128)}), f32[128,6,256]{2,0,1:T(8,128)}) %reduce-scatter.9.cloned.1.call-update) | async-done | bytes 786448 | tf_op jit(solution)/shard_map/reduce_scatter | solution.py:218
  (132 shorter events, 24.3 us)
Async XLA Ops:
  7.2 5.5 copy-start
  7.2 37.8 %copy-start.23 = (bf16[1,1024]{1,0:T(2,128)(2,1)S(1)}, bf16[1,1024]{1,0:T(2,128)(2,1)}, u32[]{:S(2)}) copy-start(bf16[1,1024]{1,0:T(2,128)(2,1)} %param.14) | copy-start | bytes 6148
  7.2 40.2 %copy-start.27 = (bf16[6,256]{1,0:T(8,128)(2,1)S(1)}, bf16[6,256]{1,0:T(8,128)(2,1)}, u32[]{:S(2)}) copy-start(bf16[6,256]{1,0:T(8,128)(2,1)} %param.16) | copy-start | bytes 9220
  7.2 37.8 %all-gather.9.cloned.1.call-start = ((), (), s32[]{:S(2)}) async-start(), calls=%async_computation.6 | async-start | bytes 3538944 | tf_op jit(solution)/shard_map/all_gather | solution.py:94
  7.9 65.4 %all-gather.11.cloned.1.call-start = ((), (), s32[]{:S(2)}) async-start(), calls=%async_computation.7 | async-start | bytes 1769472 | tf_op jit(solution)/shard_map/all_gather | solution.py:95
  9.8 81.7 %all-gather.13.cloned.1.call-start = ((), (), s32[]{:S(2)}) async-start(), calls=%async_computation.8 | async-start | bytes 3145728 | tf_op jit(solution)/shard_map/all_gather | solution.py:121
  12.7 64.1 %copy-start.14 = (f32[1024]{0:T(1024)}, f32[1024]{0:T(1024)S(1)}, u32[]{:S(2)}) copy-start(f32[1024]{0:T(1024)S(1)} %broadcast_multiply_fusion.2) | copy-start | bytes 12292
  13.3 0.6 copy-start.19
  14.0 62.9 %copy-start.21 = (f32[1024]{0:T(1024)}, f32[1024]{0:T(1024)S(1)}, u32[]{:S(2)}) copy-start(f32[1024]{0:T(1024)S(1)} %fusion.62) | copy-start | bytes 12292
  60.6 16.2 %copy-start.17 = (f32[1,1,1024]{2,1,0:T(1,128)}, f32[1,1,1024]{2,1,0:T(1,128)S(1)}, u32[]{:S(2)}) copy-start(f32[1,1,1024]{2,1,0:T(1,128)S(1)} %get-tuple-element.75) | copy-start | bytes 12292
  60.6 16.2 %copy-start.25 = (f32[1,1,1024]{2,1,0:T(1,128)}, f32[1,1,1024]{2,1,0:T(1,128)S(1)}, u32[]{:S(2)}) copy-start(f32[1,1,1024]{2,1,0:T(1,128)S(1)} %get-tuple-element.74) | copy-start | bytes 12292
  73.4 5.7 copy-start.16
  76.8 1.1 copy-start.12
  79.1 147.5 %all-reduce.5.cloned.1.call-start = ((), (), s32[]{:S(2)}) async-start(), calls=%async_computation.9 | async-start | bytes 4194304 | tf_op jit(solution)/shard_map/psum | solution.py:126
  91.4 16.0 %copy-start.3 = (bf16[1,1024,1,256]{1,3,2,0:T(8,128)(2,1)}, bf16[1,1024,1,256]{1,3,2,0:T(8,128)(2,1)S(1)}, u32[]{:S(2)}) copy-start(bf16[1,1024,1,256]{1,3,2,0:T(8,128)(2,1)S(1)} %slice.67) | copy-start | bytes 1572868
  94.4 13.1 %copy-start.6 = (bf16[2048,1,256]{0,2,1:T(8,128)(2,1)}, bf16[2048,1,256]{0,2,1:T(8,128)(2,1)S(1)}, u32[]{:S(2)}) copy-start(bf16[2048,1,256]{0,2,1:T(8,128)(2,1)S(1)} %get-tuple-element.69) | copy-start | bytes 3145732
  107.5 14.1 %copy-start.9 = (bf16[2048,1,256]{0,2,1:T(8,128)(2,1)S(1)}, bf16[2048,1,256]{0,2,1:T(8,128)(2,1)}, u32[]{:S(2)}) copy-start(bf16[2048,1,256]{0,2,1:T(8,128)(2,1)} %get-tuple-element.70) | copy-start | bytes 3145732
  136.5 4.7 copy-start.28
  136.5 4.7 copy-start.29
  139.9 115.5 %all-gather.15.cloned.1.call-start = ((), (), s32[]{:S(2)}) async-start(), calls=%async_computation.10 | async-start | bytes 2359296 | tf_op jit(solution)/shard_map/all_gather | solution.py:97
  140.5 144.7 %all-gather.17.cloned.1.call-start = ((), (), s32[]{:S(2)}) async-start(), calls=%async_computation.11 | async-start | bytes 2359296 | tf_op jit(solution)/shard_map/all_gather | solution.py:98
  141.0 244.2 %all-reduce.7.cloned.1.call-start = ((), (), s32[]{:S(2)}) async-start(), calls=%async_computation.12 | async-start | bytes 4194304 | tf_op jit(solution)/shard_map/psum | solution.py:164
  226.6 2.6 copy-start.1
  285.2 9.7 copy-start.31
  293.6 1.3 copy-start.32
  298.6 7.3 copy-start.30
  298.6 236.9 %all-gather.19.cloned.1.call-start = ((), (), s32[]{:S(2)}) async-start(), calls=%async_computation.20 | async-start | bytes 10485760 | tf_op jit(solution)/shard_map/all_gather | solution.py:135
  305.8 340.9 %reduce-scatter.7.cloned.1.call-start = ((), (), s32[]{:S(2)}) async-start(), calls=%async_computation.13 | async-start | bytes 3145728 | tf_op jit(solution)/shard_map/reduce_scatter | solution.py:178
  385.3 4.3 copy-start.2
  385.3 4.3 copy-start.8
  542.9 8.2 copy-start.11
  549.8 1.4 copy-start.5
  629.7 3.3 copy-start.7
  632.9 103.5 %all-reduce.9.cloned.1.call-start = ((), (), s32[]{:S(2)}) async-start(), calls=%async_computation.14 | async-start | bytes 4194304 | tf_op jit(solution)/shard_map/psum | solution.py:193
  651.6 139.1 %reduce-scatter.15.cloned.1.call-start = ((), (), s32[]{:S(2)}) async-start(), calls=%async_computation.18 | async-start | bytes 4718592 | tf_op jit(solution)/shard_map/reduce_scatter | solution.py:221
  658.5 187.8 %reduce-scatter.17.cloned.1.call-start = ((), (), s32[]{:S(2)}) async-start(), calls=%async_computation.19 | async-start | bytes 4718592 | tf_op jit(solution)/shard_map/reduce_scatter | solution.py:222
  666.0 1.0 copy-start.10
  666.0 4.5 copy-start.15
  666.0 4.5 copy-start.18
  666.1 4.5 copy-start.22
  666.1 4.5 copy-start.26
  666.1 220.0 %reduce-scatter.13.cloned.1.call-start = ((), (), s32[]{:S(2)}) async-start(), calls=%async_computation.17 | async-start | bytes 1179648 | tf_op jit(solution)/shard_map/reduce_scatter | solution.py:220
  670.4 5.2 copy-start.24
  670.4 265.6 %reduce-scatter.11.cloned.1.call-start = ((), (), s32[]{:S(2)}) async-start(), calls=%async_computation.16 | async-start | bytes 3538944 | tf_op jit(solution)/shard_map/reduce_scatter | solution.py:219
  675.6 63.6 %copy-start.20 = (f32[1024]{0:T(1024)S(1)}, f32[1024]{0:T(1024)}, u32[]{:S(2)}) copy-start(f32[1024]{0:T(1024)} %copy-done.19) | copy-start | bytes 12292
  675.6 326.4 %reduce-scatter.9.cloned.1.call-start = ((), (), s32[]{:S(2)}) async-start(), calls=%async_computation.15 | async-start | bytes 7077888 | tf_op jit(solution)/shard_map/reduce_scatter | solution.py:218
  736.4 2.7 copy-start.4
  745.0 1.2 copy-start.13
Sparse Core Ops, SparseCore 0:
  9.9 35.0 all-gather.8
  47.4 25.8 all-gather.10
  79.2 10.5 all-gather.12
  140.0 86.5 all-reduce.4
  228.5 26.8 all-gather.14
  257.3 27.8 all-gather.16
  298.7 86.5 all-reduce.6
  386.8 148.5 all-gather.18
  633.0 7.8 reduce-scatter.6
  651.7 84.6 all-reduce.8
  740.4 50.3 reduce-scatter.14
  794.9 51.2 reduce-scatter.16
  850.0 35.9 reduce-scatter.12
  889.8 46.1 reduce-scatter.10
  940.3 61.7 reduce-scatter.8
